TPU v7x, 32 devices: a whole 2x2x4 slice. The times are simulated.
32 devices in a mesh: row: 8 (over y, x, core), col: 4 (over z).
Axes of the slice: x: 2, y: 2, z: 4, core: 2. Of those that a mesh axis runs over, the one named last changes fastest.
Arguments:
- col_samples: float32 [16, 2, 2048, 128], P('row', None, 'col'), may hold values from -6 to 6
- row_samples: float32 [16, 2, 128, 2048], P('row', None, None, 'col'), may hold values from -6 to 6
- pivot_rows: int32 [16, 128], P('row'), may hold values from 0 to 2047
- rank_blocks: int32 [16], P('row'), may hold values from 1 to 8
- upper_inverse: float32 [2, 2048, 2048], P(None, 'col', 'row'), as said below
- upanel_left: float32 [4, 2, 2048, 128], P('col'), may hold values from -0.125 to 0.125
Outputs:
- panel_right: float32 [16, 2, 128, 2048], P('row', None, None, 'col')
- cores: float32 [16, 4, 2, 128, 128], P('row', 'col')
Inputs may be any that keep to these rules, and one draw needn't show every extreme that they name: `rank_blocks`: the tile's rank is 16 times this. `upper_inverse`: zero below the diagonal in both parts.
All inputs are finite; a program needn't handle non-finite values.
Results may differ from a plain program's by a relative error of at most 0.00007.
Values sent between devices are 32-bit elements; how exact they have to be, the bound alone decides.
A program may use at most 64 MiB of HBM per device.

v0:
```python
import jax
import jax.numpy as jnp
from jax import lax
from jax.sharding import PartitionSpec as P

RANK_STEP = 16


def complex_product(pattern, left_real, left_imag, right_real, right_imag):

    def single(left, right):
        return jnp.einsum(
            pattern,
            left,
            right,
            precision=lax.Precision.HIGHEST,
            preferred_element_type=jnp.float32,
        )

    real_part = single(left_real, right_real) - single(left_imag, right_imag)
    imag_part = single(left_real, right_imag) + single(left_imag, right_real)
    return (real_part, imag_part)


def scale_rows(values, weight_real, weight_imag):
    wr = weight_real[:, :, None]
    wi = weight_imag[:, :, None]
    real_part = values[:, 0] * wr - values[:, 1] * wi
    imag_part = values[:, 0] * wi + values[:, 1] * wr
    return jnp.stack((real_part, imag_part), axis=1)


def on_device(col_samples, row_samples, pivot_rows, rank_blocks, upper_inverse, upanel_left):
    width_local = col_samples.shape[2]
    ranks_max = row_samples.shape[2]
    offset = lax.axis_index("col") * width_local
    positions = offset + lax.broadcasted_iota(jnp.int32, (1, 1, width_local), 2)
    hits = (pivot_rows[:, :, None] == positions).astype(jnp.float32)
    flipped = jnp.swapaxes(col_samples, 2, 3)
    partial_entries = jnp.sum(flipped * hits[:, None], axis=3)
    entries = lax.psum(partial_entries, "col")
    levels = lax.broadcasted_iota(jnp.int32, (1, ranks_max), 1)
    keeping = (levels < RANK_STEP * rank_blocks[:, None]).astype(jnp.float32)
    magnitude = jnp.maximum(entries[:, 0] * entries[:, 0] + entries[:, 1] * entries[:, 1], 1.0)
    factor_real = keeping * entries[:, 0] / magnitude
    factor_imag = -keeping * entries[:, 1] / magnitude
    scaled = scale_rows(row_samples, factor_real, factor_imag)
    portion = lax.all_gather(upper_inverse, "row", axis=2, tiled=True)
    real_part, imag_part = complex_product(
        "trk,kn->trn", scaled[:, 0], scaled[:, 1], portion[0], portion[1]
    )
    partial_panel = jnp.stack((real_part, imag_part), axis=1)
    panel_full = lax.psum(partial_panel, "col")
    core_real, core_imag = complex_product(
        "trn,jns->tjrs", panel_full[:, 0], panel_full[:, 1], upanel_left[:, 0], upanel_left[:, 1]
    )
    cores = jnp.stack((core_real, core_imag), axis=2)
    panel_local = lax.dynamic_slice_in_dim(panel_full, offset, width_local, 3)
    return (panel_local, cores)


def solution(mesh):
    in_specs = (
        P("row", None, "col", None),
        P("row", None, None, "col"),
        P("row", None),
        P("row"),
        P(None, "col", "row"),
        P("col", None, None, None),
    )
    out_specs = (P("row", None, None, "col"), P("row", "col", None, None, None))
    return jax.shard_map(
        on_device, mesh=mesh, in_specs=in_specs, out_specs=out_specs, check_vma=False
    )
```

profile of v0, /device:TPU:0, one launch (start us, length us, event | category | flops | bytes accessed | tf_op | source)
XLA Modules:
  0.0 263.2 jit_solution(7308855048611063219)
XLA Ops:
  7.2 0.0 all-gather.2.cloned.1.call-start
  7.2 0.7 all-gather.2.cloned.1.call-update
  7.9 0.0 all-reduce.2.cloned.1.call-start
  8.0 0.8 compare_convert_fusion
  8.8 0.0 copy-start.3
  8.8 1.4 fusion.20
  10.2 13.5 %psum.14 = f32[2,2,128]{2,1,0:T(2,128)S(1)} all-reduce(f32[2,2,128]{2,1,0:T(2,128)S(1)} %fusion.20), channel_id=1, replica_groups=mesh['row'=8,'col'=4] {'col'}, use_global_device_ids=true, to_apply=%region_1.0 | all-reduce | flops 512 | bytes 4096 | tf_op jit(solution)/shard_map/psum | solution.py:41
  23.7 0.7 broadcast_multiply_fusion
  24.3 0.1 select_divide_fusion
  24.4 44.1 %all-gather.2.cloned.1.call-done = f32[2,512,2048]{2,1,0:T(8,128)} async-done(((f32[2,512,256]{2,1,0:T(8,128)}), f32[2,512,2048]{2,1,0:T(8,128)}) %all-gather.2.cloned.1.call-update) | async-done | bytes 8388624 | tf_op jit(solution)/shard_map/all_gather | solution.py:48
  68.5 0.0 copy-start
  68.5 5.9 %fusion = f32[2,128,2048]{2,1,0:T(8,128)S(1)} fusion(f32[2,512,2048]{2,1,0:T(8,128)} %all-gather.2.cloned.1.call-done, f32[2,2,128,512]{3,2,1,0:T(8,128)} %param.7, f32[2,128]{1,0:T(2,128)S(1)} %get-tuple-element.7, f32[2,128]{1,0:T(2,128)S(1)} %get-tuple-element.6), kind=kOutput, calls=%fused_computation.3 | convolution fusion | flops 3221618688 | bytes 7342080 | tf_op jit(solution)/shard_map/trk,kn->trn/dot_general | solution.py:12
  74.4 0.0 copy-done.3
  74.4 5.7 %fusion.1 = f32[2,128,2048]{2,1,0:T(8,128)S(1)} fusion(f32[2,512,2048]{2,1,0:T(8,128)} %all-gather.2.cloned.1.call-done, f32[2,2,128,512]{3,2,1,0:T(8,128)S(1)} %copy-done.3, f32[2,128]{1,0:T(2,128)S(1)} %get-tuple-element.7, f32[2,128]{1,0:T(2,128)S(1)} %get-tuple-element.6), kind=kOutput, calls=%fused_computation.4 | convolution fusion | flops 3221618688 | bytes 7342080 | tf_op jit(solution)/shard_map/trk,kn->trn/dot_general | solution.py:12
  80.1 0.0 copy-done
  80.1 3.8 %fusion.7 = f32[2,1,128,2048]{3,2,0,1:T(8,128)S(1)} fusion(f32[2,128,2048]{2,1,0:T(8,128)S(1)} %fusion, f32[2,512,2048]{2,1,0:T(8,128)S(1)} %copy-done, f32[2,2,128,512]{3,2,1,0:T(8,128)S(1)} %copy-done.3, f32[2,128]{1,0:T(2,128)S(1)} %get-tuple-element.7, f32[2,128]{1,0:T(2,128)S(1)} %get-tuple-element.6), kind=kOutput, calls=%fused_computation.10 | convolution fusion | flops 3222142976 | bytes 9439232 | tf_op jit(solution)/shard_map/trk,kn->trn/dot_general | solution.py:12
  84.0 3.8 %fusion.5 = f32[2,1,128,2048]{3,2,0,1:T(8,128)S(1)} fusion(f32[2,128,2048]{2,1,0:T(8,128)S(1)} %fusion.1, f32[2,512,2048]{2,1,0:T(8,128)S(1)} %copy-done, f32[2,2,128,512]{3,2,1,0:T(8,128)S(1)} %copy-done.3, f32[2,128]{1,0:T(2,128)S(1)} %get-tuple-element.7, f32[2,128]{1,0:T(2,128)S(1)} %get-tuple-element.6), kind=kOutput, calls=%fused_computation.8 | convolution fusion | flops 3222142976 | bytes 9439232 | tf_op jit(solution)/shard_map/trk,kn->trn/dot_general | solution.py:12
  87.8 2.5 pad_maximum_fusion
  90.2 0.0 copy-start.2
  90.2 0.0 all-reduce.2.cloned.1.call-update
  90.3 155.1 %all-reduce.2.cloned.1.call-done = f32[2,2,128,2048]{3,2,0,1:T(8,128)} async-done(((f32[2,2,128,2048]{3,2,0,1:T(8,128)}), f32[2,2,128,2048]{3,2,0,1:T(8,128)}) %all-reduce.2.cloned.1.call-update) | async-done | bytes 4194320 | tf_op jit(solution)/shard_map/psum | solution.py:53
  245.4 0.0 copy-start.1
  245.4 1.4 constant_dynamic-slice_fusion
  246.8 1.0 copy.11
  247.9 0.0 copy-done.2
  247.9 0.1 copy-done.1
  248.0 1.8 fusion.8
  249.8 1.8 fusion.9
  251.7 2.1 fusion.15
  253.8 1.8 fusion.13
  255.6 0.7 copy.12
  (3 shorter events, 0.0 us)
Async XLA Ops:
  7.2 61.3 %all-gather.2.cloned.1.call-start = ((), (), s32[]{:S(2)}) async-start(), calls=%async_computation | async-start | bytes 9437184 | tf_op jit(solution)/shard_map/all_gather | solution.py:48
  7.9 237.5 %all-reduce.2.cloned.1.call-start = ((), (), s32[]{:S(2)}) async-start(), calls=%async_computation.1 | async-start | bytes 8388608 | tf_op jit(solution)/shard_map/psum | solution.py:53
  8.8 65.6 %copy-start.3 = (f32[2,2,128,512]{3,2,1,0:T(8,128)S(1)}, f32[2,2,128,512]{3,2,1,0:T(8,128)}, u32[]{:S(2)}) copy-start(f32[2,2,128,512]{3,2,1,0:T(8,128)} %param.7) | copy-start | bytes 3145732
  68.5 11.7 %copy-start = (f32[2,512,2048]{2,1,0:T(8,128)S(1)}, f32[2,512,2048]{2,1,0:T(8,128)}, u32[]{:S(2)}) copy-start(f32[2,512,2048]{2,1,0:T(8,128)} %all-gather.2.cloned.1.call-done) | copy-start | bytes 25165828
  90.2 157.6 %copy-start.2 = (f32[1,2,2048,128]{3,2,1,0:T(8,128)S(1)}, f32[1,2,2048,128]{3,2,1,0:T(8,128)}, u32[]{:S(2)}) copy-start(f32[1,2,2048,128]{3,2,1,0:T(8,128)} %param.11) | copy-start | bytes 6291460
  245.4 2.6 copy-start.1
Sparse Core Ops, SparseCore 0:
  9.8 58.5 all-gather.1
  90.4 154.9 all-reduce.1
where the time goes:
time: 263 us
  waiting for transfers between devices  200 us (76%)
  matrix products  26.8 us (10%)
  between operations  14.2 us (5%)
  blocking collectives  13.5 us (5%)
  other arithmetic  5.43 us (2%)
  local copies, waits for them, and re-layouts  3.36 us (1%)
    psum x1, waiting for transfers between devices, on_device(): panel_full = lax.psum(partial_panel, 'col')  155 us
    all_gather x1, waiting for transfers between devices, on_device(): portion = lax.all_gather(upper_inverse, 'row', axis=2, tiled=True)  44.1 us
    dot_general x8, matrix products, single(): jnp.einsum(pattern, left, right, precision=lax.Precision.HIGHEST, preferr...  26.8 us
    psum x1, blocking collectives, on_device(): entries = lax.psum(partial_entries, 'col')  13.5 us
  transfers between devices with their start and end apart: 2, of which 2 were waited for; matrix products, arithmetic and copies ran while one was open for 1% of the time, Pallas kernels for 0%

commit v1 on v0

--- a/solution.py
+++ b/solution.py
@@ -50,7 +50,7 @@
         "trk,kn->trn", scaled[:, 0], scaled[:, 1], portion[0], portion[1]
     )
     partial_panel = jnp.stack((real_part, imag_part), axis=1)
-    panel_full = lax.psum(partial_panel, "col")
+    panel_full = jnp.sum(lax.all_gather(partial_panel, "col"), axis=0)
     core_real, core_imag = complex_product(
         "trn,jns->tjrs", panel_full[:, 0], panel_full[:, 1], upanel_left[:, 0], upanel_left[:, 1]
     )

time: 263 us -> 407 us (1.55)
  waiting for transfers between devices: 200 us -> 332 us
  other arithmetic: 5.43 us -> 15.7 us
    all_gather x0 -> x1, waiting for transfers between devices: none -> 287 us  [on_device(): panel_full = jnp.sum(lax.all_gather(partial_panel, 'col'), axis=0)]
    psum x1 -> x0, waiting for transfers between devices: 155 us -> none  [on_device(): panel_full = lax.psum(partial_panel, 'col')]
    reduce_sum x0 -> x1, other arithmetic: none -> 10.3 us  [on_device(): panel_full = jnp.sum(lax.all_gather(partial_panel, 'col'), axis=0)]
where the time goes in v1:
time: 407 us
  waiting for transfers between devices  332 us (82%)
  matrix products  30.1 us (7%)
  other arithmetic  15.7 us (4%)
  between operations  14.2 us (3%)
  blocking collectives  13.5 us (3%)
    all_gather x1, waiting for transfers between devices, on_device(): panel_full = jnp.sum(lax.all_gather(partial_panel, 'col'), axis=0)  287 us
    all_gather x1, waiting for transfers between devices, on_device(): portion = lax.all_gather(upper_inverse, 'row', axis=2, tiled=True)  44.1 us
    dot_general x8, matrix products, single(): jnp.einsum(pattern, left, right, precision=lax.Precision.HIGHEST, preferr...  30.1 us
    psum x1, blocking collectives, on_device(): entries = lax.psum(partial_entries, 'col')  13.5 us
    reduce_sum x1, other arithmetic, on_device(): panel_full = jnp.sum(lax.all_gather(partial_panel, 'col'), axis=0)  10.3 us
  transfers between devices with their start and end apart: 2, of which 2 were waited for; matrix products, arithmetic and copies ran while one was open for 1% of the time, Pallas kernels for 0%

profile of v1, /device:TPU:0, one launch (start us, length us, event | category | flops | bytes accessed | tf_op | source)
XLA Modules:
  0.0 407.1 jit_solution(6345910337277277794)
XLA Ops:
  7.2 0.0 all-gather.4.cloned.1.call-start
  7.2 0.7 all-gather.4.cloned.1.call-update
  7.9 0.0 all-gather.6.cloned.1.call-start
  8.0 0.8 compare_convert_fusion
  8.8 0.0 copy-start.3
  8.8 1.4 fusion.20
  10.2 13.5 %psum.7 = f32[2,2,128]{2,1,0:T(2,128)S(1)} all-reduce(f32[2,2,128]{2,1,0:T(2,128)S(1)} %fusion.20), channel_id=1, replica_groups=mesh['row'=8,'col'=4] {'col'}, use_global_device_ids=true, to_apply=%region_1.0 | all-reduce | flops 512 | bytes 4096 | tf_op jit(solution)/shard_map/psum | solution.py:41
  23.7 0.7 broadcast_multiply_fusion
  24.3 0.1 select_divide_fusion
  24.4 44.1 %all-gather.4.cloned.1.call-done = f32[2,512,2048]{2,1,0:T(8,128)} async-done(((f32[2,512,256]{2,1,0:T(8,128)}), f32[2,512,2048]{2,1,0:T(8,128)}) %all-gather.4.cloned.1.call-update) | async-done | bytes 8388624 | tf_op jit(solution)/shard_map/all_gather | solution.py:48
  68.5 0.0 copy-start.1
  68.5 5.9 %fusion = f32[2,128,2048]{2,1,0:T(8,128)S(1)} fusion(f32[2,512,2048]{2,1,0:T(8,128)} %all-gather.4.cloned.1.call-done, f32[2,2,128,512]{3,2,1,0:T(8,128)} %param.7, f32[2,128]{1,0:T(2,128)S(1)} %get-tuple-element.7, f32[2,128]{1,0:T(2,128)S(1)} %get-tuple-element.6), kind=kOutput, calls=%fused_computation.3 | convolution fusion | flops 3221618688 | bytes 7342080 | tf_op jit(solution)/shard_map/trk,kn->trn/dot_general | solution.py:12
  74.4 0.0 copy-done.3
  74.4 5.7 %fusion.1 = f32[2,128,2048]{2,1,0:T(8,128)S(1)} fusion(f32[2,512,2048]{2,1,0:T(8,128)} %all-gather.4.cloned.1.call-done, f32[2,2,128,512]{3,2,1,0:T(8,128)S(1)} %copy-done.3, f32[2,128]{1,0:T(2,128)S(1)} %get-tuple-element.7, f32[2,128]{1,0:T(2,128)S(1)} %get-tuple-element.6), kind=kOutput, calls=%fused_computation.4 | convolution fusion | flops 3221618688 | bytes 7342080 | tf_op jit(solution)/shard_map/trk,kn->trn/dot_general | solution.py:12
  80.1 0.0 copy-done.1
  80.1 3.8 fusion.7
  84.0 3.8 fusion.5
  87.8 2.4 pad_maximum_fusion
  90.2 0.0 all-gather.6.cloned.1.call-update
  90.2 286.9 %all-gather.6.cloned.1.call-done = f32[8,2,128,2048]{3,2,0,1:T(8,128)} async-done(((f32[2,2,128,2048]{3,2,0,1:T(8,128)}), f32[8,2,128,2048]{3,2,0,1:T(8,128)}) %all-gather.6.cloned.1.call-update) | async-done | bytes 16777232 | tf_op jit(solution)/shard_map/all_gather | solution.py:53
  377.1 0.0 copy-start.2
  377.1 10.3 %reduce_sum.19 = f32[2,2,128,2048]{3,2,0,1:T(8,128)} reduce(f32[4,2,2,128,2048]{4,3,1,0,2:T(8,128)} %bitcast.87, f32[]{:T(128)} %constant.4.clone.1), dimensions={0}, to_apply=%region_2.0 | reduce | flops 3145728 | bytes 20971524 | tf_op jit(solution)/shard_map/reduce_sum | solution.py:53
  387.4 0.0 copy-done.2
  387.4 0.0 copy-start
  387.4 3.5 fusion.8
  391.0 3.6 fusion.9
  394.6 0.0 copy-done
  394.6 1.8 fusion.15
  396.5 1.8 fusion.13
  398.3 0.1 constant_dynamic-slice_fusion
  398.4 1.0 copy.11
  399.5 0.7 copy.12
  (3 shorter events, 0.0 us)
Async XLA Ops:
  7.2 61.3 %all-gather.4.cloned.1.call-start = ((), (), s32[]{:S(2)}) async-start(), calls=%async_computation | async-start | bytes 9437184 | tf_op jit(solution)/shard_map/all_gather | solution.py:48
  7.9 369.2 %all-gather.6.cloned.1.call-start = ((), (), s32[]{:S(2)}) async-start(), calls=%async_computation.1 | async-start | bytes 20971520 | tf_op jit(solution)/shard_map/all_gather | solution.py:53
  8.8 65.6 %copy-start.3 = (f32[2,2,128,512]{3,2,1,0:T(8,128)S(1)}, f32[2,2,128,512]{3,2,1,0:T(8,128)}, u32[]{:S(2)}) copy-start(f32[2,2,128,512]{3,2,1,0:T(8,128)} %param.7) | copy-start | bytes 3145732
  68.5 11.7 %copy-start.1 = (f32[2,512,2048]{2,1,0:T(8,128)S(1)}, f32[2,512,2048]{2,1,0:T(8,128)}, u32[]{:S(2)}) copy-start(f32[2,512,2048]{2,1,0:T(8,128)} %all-gather.4.cloned.1.call-done) | copy-start | bytes 25165828
  377.1 10.3 %copy-start.2 = (f32[1,2,2048,128]{3,2,1,0:T(8,128)S(1)}, f32[1,2,2048,128]{3,2,1,0:T(8,128)}, u32[]{:S(2)}) copy-start(f32[1,2,2048,128]{3,2,1,0:T(8,128)} %param.11) | copy-start | bytes 6291460
  387.4 7.2 %copy-start = (f32[2,2,128,2048]{3,2,0,1:T(8,128)S(1)}, f32[2,2,128,2048]{3,2,0,1:T(8,128)}, u32[]{:S(2)}) copy-start(f32[2,2,128,2048]{3,2,0,1:T(8,128)} %reduce_sum.19) | copy-start | bytes 12582916
Sparse Core Ops, SparseCore 0:
  9.8 58.5 all-gather.3
  90.4 286.7 all-gather.5
